TPU v7x, 256 devices: a whole 4x4x8 slice. The times are simulated.
256 devices in a mesh: rep: 8 (over y, x_hi), blk: 32 (over z, x_lo, core).
Axes of the slice: x: 4 (x_hi: 2, x_lo: 2; x = x_hi * 2 + x_lo), y: 4, z: 8, core: 2. Of those that a mesh axis runs over, the one named last changes fastest.
Arguments:
- node_features: bfloat16 [65536, 256], P(('rep', 'blk')), may hold values from -6 to 6
- tile_values: bfloat16 [8, 32, 128, 128, 128], P('rep', 'blk'), may hold values from -0.09375 to 0.09375
- tile_row: int32 [8, 32, 128], P('rep', 'blk'), may hold values from 0 to 15, as said below
- tile_col: int32 [8, 32, 128], P('rep', 'blk'), may hold values from 0 to 63
- tile_count: int32 [8, 32], P('rep', 'blk'), may hold values from 16 to 128, as said below
- weight: bfloat16 [256, 256], replicated, may hold values from -0.375 to 0.375
- cotangent: bfloat16 [32, 8, 256, 256], P('blk', 'rep'), may hold values from -6 to 6
Outputs:
- layer_out: bfloat16 [32, 8, 256, 256], P('blk', 'rep')
- grad_weight: float32 [256, 256], replicated
- grad_features: bfloat16 [65536, 256], P(('rep', 'blk'))
Inputs may be any that keep to these rules, and one draw needn't show every extreme that they name: `tile_row`: within one device the live slots name distinct tile pairs. Slots 0 to tile_count - 1 of a device are live, the rest are ignored; some device has all 128 slots live.
All inputs are finite; a program needn't handle non-finite values.
Results may differ from a plain program's by a relative error of at most 0.03.
Values may be sent and summed in bfloat16 or wider, within the bound.
No kernel may reach another device: no remote copies, remote signals or barrier semaphores. Data moves between devices by JAX's collectives and lax.ppermute only.
A program may use at most 128 MiB of HBM per device.

v0:
```python
import jax
import jax.numpy as jnp
from jax import lax
from jax.sharding import PartitionSpec as P


def on_device(node_features, tile_values, tile_row, tile_col, tile_count, weight, cotangent):
    rows_dev, features = node_features.shape
    tile_block = tile_values[0, 0]
    slot_rows = tile_row[0, 0]
    slot_cols = tile_col[0, 0]
    live_count = tile_count[0, 0]
    slot_count = tile_block.shape[0]
    tile_size = tile_block.shape[1]
    rep_size = lax.axis_size("rep")
    slab_rows = rows_dev * rep_size
    slab_blocks = slab_rows // tile_size
    live_mask = (jnp.arange(slot_count, dtype=jnp.int32) < live_count).astype(jnp.float32)
    row_hot = (slot_rows[:, None] == jnp.arange(slab_blocks, dtype=jnp.int32)[None, :]).astype(
        jnp.float32
    ) * live_mask[:, None]
    gathered = lax.all_gather(node_features, "blk", axis=0, tiled=True)
    group_blocks = gathered.shape[0] // tile_size
    col_hot = (slot_cols[:, None] == jnp.arange(group_blocks, dtype=jnp.int32)[None, :]).astype(
        jnp.float32
    ) * live_mask[:, None]
    col_blocks = gathered.reshape(group_blocks, tile_size, features)
    picked = jnp.take(col_blocks, slot_cols, axis=0)
    products = jnp.einsum("tij,tjf->tif", tile_block, picked, preferred_element_type=jnp.float32)
    partial_value = (
        jnp.einsum("tk,tif->kif", row_hot, products)
        .reshape(slab_rows, features)
        .astype(jnp.bfloat16)
    )
    hidden_rows = (
        lax.psum_scatter(partial_value, "rep", scatter_dimension=0, tiled=True)
        .astype(jnp.float32)
        .astype(jnp.bfloat16)
    )
    preact = jnp.dot(hidden_rows, weight, preferred_element_type=jnp.float32)
    gating = jax.nn.sigmoid(preact)
    layer_out = (preact * gating).astype(jnp.bfloat16)
    slope_term = gating * (1.0 + preact * (1.0 - gating))
    grad_pre = (cotangent[0, 0].astype(jnp.float32) * slope_term).astype(jnp.bfloat16)
    weight_part = jnp.einsum("nf,ng->fg", hidden_rows, grad_pre, preferred_element_type=jnp.float32)
    grad_hidden = jnp.dot(grad_pre, weight.T, preferred_element_type=jnp.float32).astype(
        jnp.bfloat16
    )
    grad_slab = lax.all_gather(grad_hidden, "rep", axis=0, tiled=True)
    grad_weight = lax.psum(weight_part, ("rep", "blk"))
    grad_blocks = grad_slab.reshape(slab_blocks, tile_size, features)
    picked_rows = jnp.take(grad_blocks, slot_rows, axis=0)
    back_terms = jnp.einsum(
        "tij,tif->tjf", tile_block, picked_rows, preferred_element_type=jnp.float32
    )
    column_terms = (
        jnp.einsum("tk,tjf->kjf", col_hot, back_terms)
        .reshape(group_blocks * tile_size, features)
        .astype(jnp.bfloat16)
    )
    grad_features = (
        lax.psum_scatter(column_terms, "blk", scatter_dimension=0, tiled=True)
        .astype(jnp.float32)
        .astype(jnp.bfloat16)
    )
    return (layer_out.reshape(1, 1, rows_dev, features), grad_weight, grad_features)


def solution(mesh):
    placed = (
        P(("rep", "blk"), None),
        P("rep", "blk", None, None, None),
        P("rep", "blk", None),
        P("rep", "blk", None),
        P("rep", "blk"),
        P(),
        P("blk", "rep", None, None),
    )
    return jax.shard_map(
        on_device,
        mesh=mesh,
        in_specs=placed,
        out_specs=(P("blk", "rep", None, None), P(), P(("rep", "blk"), None)),
        check_vma=False,
    )
```

profile of v0, /device:TPU:24, one launch (start us, length us, event | category | flops | bytes accessed | tf_op | source)
XLA Modules:
  0.0 638.3 jit_solution(16897174415970150977)
XLA Ops:
  7.2 0.0 copy-start
  7.2 0.0 all-gather.3.cloned.1.call-start
  7.2 0.7 all-gather.3.cloned.1.call-update
  7.9 0.0 reduce-scatter.3.cloned.1.call-start
  8.6 0.7 fusion.32
  9.3 0.7 compare_and_fusion.1
  9.9 69.5 %all-gather.3.cloned.1.call-done = bf16[8192,256]{1,0:T(8,128)(2,1)} async-done(((bf16[256,256]{1,0:T(8,128)(2,1)}), bf16[8192,256]{1,0:T(8,128)(2,1)}) %all-gather.3.cloned.1.call-update) | async-done | bytes 4194320 | tf_op jit(solution)/shard_map/all_gather | solution.py:22
  79.4 8.8 %gather_fusion = bf16[128,128,256]{2,1,0:T(8,128)(2,1)} fusion(bf16[64,128,256]{2,1,0:T(8,128)(2,1)} %bitcast.51, s32[1024]{0:T(1024)S(1)} %pad_clamp_fusion.1), kind=kCustom, calls=%fused_computation | custom fusion | bytes 16777728 | tf_op jit(solution)/shard_map/jit(_take)/gather | solution.py:28
  88.2 11.9 %fusion.6 = bf16[128,256,128]{2,1,0:T(8,128)(2,1)} fusion(bf16[128,128,256]{2,1,0:T(8,128)(2,1)} %gather_fusion, pred[128]{0:T(512)(128)(4,1)S(1)} %compare_and_fusion.1, bf16[1,1,128,128,128]{4,3,2,1,0:T(8,128)(2,1)} %param.8), kind=kOutput, calls=%fused_computation.8 | convolution fusion | flops 1077936128 | bytes 20971648 | tf_op jit(solution)/shard_map/tij,tjf->tif/dot_general | solution.py:29
  100.1 0.0 copy-start.2
  100.1 12.4 %copy.12 = bf16[128,256,128]{1,0,2:T(8,128)(2,1)} copy(bf16[128,256,128]{2,1,0:T(8,128)(2,1)} %fusion.6) | data formatting | bytes 16777216 | tf_op jit(solution)/shard_map/tij,tjf->tif/dot_general | solution.py:29
  112.5 0.0 copy-start.4
  112.5 0.0 copy-done.2
  112.5 4.6 fusion.17
  117.1 1.4 copy.10
  118.4 0.0 reduce-scatter.3.cloned.1.call-update
  118.5 0.0 all-gather.5.cloned.1.call-start
  118.5 76.1 %reduce-scatter.3.cloned.1.call-done = bf16[256,256]{1,0:T(8,128)(2,1)} async-done(((bf16[2048,256]{1,0:T(8,128)(2,1)}), bf16[256,256]{1,0:T(8,128)(2,1)}) %reduce-scatter.3.cloned.1.call-update) | async-done | bytes 131088 | tf_op jit(solution)/shard_map/reduce_scatter | solution.py:36
  194.6 0.0 copy-done
  194.6 0.0 copy-done.4
  194.6 1.8 fusion.20
  196.5 0.9 convolution_convert_fusion
  197.4 0.0 all-gather.5.cloned.1.call-update
  197.4 0.0 all-reduce.2.cloned.1.call-start
  197.5 1.8 fusion.38
  199.3 0.0 all-reduce.2.cloned.1.call-update
  199.3 0.2 reduce-scatter.5.cloned.1.call-start
  199.6 49.1 %all-gather.5.cloned.1.call-done = bf16[2048,256]{1,0:T(8,128)(2,1)} async-done(((bf16[256,256]{1,0:T(8,128)(2,1)}), bf16[2048,256]{1,0:T(8,128)(2,1)}) %all-gather.5.cloned.1.call-update) | async-done | bytes 1048592 | tf_op jit(solution)/shard_map/all_gather | solution.py:49
  248.7 7.8 %gather_fusion.1 = bf16[128,128,256]{2,1,0:T(8,128)(2,1)} fusion(bf16[16,128,256]{2,1,0:T(8,128)(2,1)} %bitcast.50, s32[1024]{0:T(1024)S(1)} %pad_clamp_fusion), kind=kCustom, calls=%fused_computation.1 | custom fusion | bytes 16777728 | tf_op jit(solution)/shard_map/jit(_take)/gather | solution.py:52
  256.5 8.9 %fusion.4 = bf16[128,256,128]{2,1,0:T(8,128)(2,1)} fusion(bf16[128,128,256]{2,1,0:T(8,128)(2,1)} %gather_fusion.1, pred[128]{0:T(512)(128)(4,1)S(1)} %compare_and_fusion, bf16[1,1,128,128,128]{4,3,2,1,0:T(8,128)(2,1)} %param.8), kind=kOutput, calls=%fused_computation.6 | convolution fusion | flops 1077936128 | bytes 20971648 | tf_op jit(solution)/shard_map/tij,tif->tjf/dot_general | solution.py:53
  265.4 0.0 copy-start.3
  265.4 12.5 %copy.13 = bf16[128,256,128]{1,0,2:T(8,128)(2,1)} copy(bf16[128,256,128]{2,1,0:T(8,128)(2,1)} %fusion.4) | data formatting | bytes 16777216 | tf_op jit(solution)/shard_map/tij,tif->tjf/dot_general | solution.py:53
  277.8 0.0 copy-done.3
  277.8 0.0 copy-start.1
  277.8 4.7 fusion.14
  282.6 4.4 copy.11
  287.0 0.0 reduce-scatter.5.cloned.1.call-update
  287.0 217.9 %all-reduce.2.cloned.1.call-done = f32[256,256]{1,0:T(8,128)} async-done(((f32[256,256]{1,0:T(8,128)}), f32[256,256]{1,0:T(8,128)}) %all-reduce.2.cloned.1.call-update) | async-done | bytes 262160 | tf_op jit(solution)/shard_map/psum | solution.py:50
  504.9 125.2 %reduce-scatter.5.cloned.1.call-done = bf16[256,256]{1,0:T(8,128)(2,1)} async-done(((bf16[8192,256]{1,0:T(8,128)(2,1)}), bf16[256,256]{1,0:T(8,128)(2,1)}) %reduce-scatter.5.cloned.1.call-update) | async-done | bytes 131088 | tf_op jit(solution)/shard_map/reduce_scatter | solution.py:62
  630.1 1.7 copy.16
  631.7 0.0 copy-done.1
  (5 shorter events, 0.0 us)
Async XLA Ops:
  7.2 187.5 %copy-start = (bf16[256,256]{1,0:T(8,128)(2,1)S(1)}, bf16[256,256]{1,0:T(8,128)(2,1)}, u32[]{:S(2)}) copy-start(bf16[256,256]{1,0:T(8,128)(2,1)} %param.12) | copy-start | bytes 393220
  7.2 72.2 %all-gather.3.cloned.1.call-start = ((), (), s32[]{:S(2)}) async-start(), calls=%async_computation.2 | async-start | bytes 4325376 | tf_op jit(solution)/shard_map/all_gather | solution.py:22
  7.9 186.7 %reduce-scatter.3.cloned.1.call-start = ((), (), s32[]{:S(2)}) async-start(), calls=%async_computation.3 | async-start | bytes 1179648 | tf_op jit(solution)/shard_map/reduce_scatter | solution.py:36
  100.1 12.4 %copy-start.2 = (s32[1,1,128]{2,1,0:T(1,128)S(1)}, s32[1,1,128]{2,1,0:T(1,128)}, u32[]{:S(2)}) copy-start(s32[1,1,128]{2,1,0:T(1,128)} %param.9) | copy-start | bytes 1540
  112.5 82.2 %copy-start.4 = (bf16[1,1,256,256]{3,2,1,0:T(8,128)(2,1)S(1)}, bf16[1,1,256,256]{3,2,1,0:T(8,128)(2,1)}, u32[]{:S(2)}) copy-start(bf16[1,1,256,256]{3,2,1,0:T(8,128)(2,1)} %param.13) | copy-start | bytes 393220
  118.5 130.2 %all-gather.5.cloned.1.call-start = ((), (), s32[]{:S(2)}) async-start(), calls=%async_computation.5 | async-start | bytes 1179648 | tf_op jit(solution)/shard_map/all_gather | solution.py:49
  197.4 307.5 %all-reduce.2.cloned.1.call-start = ((), (), s32[]{:S(2)}) async-start(), calls=%async_computation.4 | async-start | bytes 524288 | tf_op jit(solution)/shard_map/psum | solution.py:50
  199.3 430.7 %reduce-scatter.5.cloned.1.call-start = ((), (), s32[]{:S(2)}) async-start(), calls=%async_computation.6 | async-start | bytes 4325376 | tf_op jit(solution)/shard_map/reduce_scatter | solution.py:62
  265.4 12.5 %copy-start.3 = (s32[1,1,128]{2,1,0:T(1,128)S(1)}, s32[1,1,128]{2,1,0:T(1,128)}, u32[]{:S(2)}) copy-start(s32[1,1,128]{2,1,0:T(1,128)} %param.10) | copy-start | bytes 1540
  277.8 353.9 %copy-start.1 = (bf16[256,256]{1,0:T(8,128)(2,1)S(1)}, bf16[256,256]{1,0:T(8,128)(2,1)}, u32[]{:S(2)}) copy-start(bf16[256,256]{1,0:T(8,128)(2,1)} %param.12) | copy-start | bytes 393220
Sparse Core Ops, SparseCore 0:
  9.9 69.5 all-gather.2
  118.6 76.0 reduce-scatter.2
  198.2 50.4 all-gather.4
  255.5 249.3 all-reduce.1
  508.0 122.0 reduce-scatter.4
where the time goes:
time: 639 us; the launch traced here: 638 us
  waiting for transfers between devices  539 us (84%)
  local copies, waits for them, and re-layouts  48.8 us (8%)
  matrix products  34.7 us (5%)
  between operations  14.5 us (2%)
    psum x1, waiting for transfers between devices, on_device(): grad_weight = lax.psum(weight_part, ('rep', 'blk'))  218 us
    reduce_scatter x1, waiting for transfers between devices, on_device(): lax.psum_scatter(column_terms, 'blk', scatter_dimension=0, tiled=True)  125 us
    reduce_scatter x1, waiting for transfers between devices, on_device(): lax.psum_scatter(partial_value, 'rep', scatter_dimension=0, tiled=True)  76.1 us
    all_gather x1, waiting for transfers between devices, on_device(): gathered = lax.all_gather(node_features, 'blk', axis=0, tiled=True)  69.5 us
    all_gather x1, waiting for transfers between devices, on_device(): grad_slab = lax.all_gather(grad_hidden, 'rep', axis=0, tiled=True)  49.1 us
  transfers between devices with their start and end apart: 5, of which 5 were waited for; matrix products, arithmetic and copies ran while one was open for 6% of the time, Pallas kernels for 0%

commit v1 on v0

--- a/solution.py
+++ b/solution.py
@@ -46,7 +46,8 @@
     grad_hidden = jnp.dot(grad_pre, weight.T, preferred_element_type=jnp.float32).astype(
         jnp.bfloat16
     )
-    grad_slab = lax.all_gather(grad_hidden, "rep", axis=0, tiled=True)
+    sent = jnp.stack([grad_hidden] * lax.axis_size("rep"))
+    grad_slab = jnp.concatenate(lax.all_to_all(sent, "rep", 0, 0), axis=0)
     grad_weight = lax.psum(weight_part, ("rep", "blk"))
     grad_blocks = grad_slab.reshape(slab_blocks, tile_size, features)
     picked_rows = jnp.take(grad_blocks, slot_rows, axis=0)

time: 639 us -> 596 us (0.933)
  waiting for transfers between devices: 539 us -> 491 us
    all_gather x1 -> x0, waiting for transfers between devices: 49.1 us -> none  [on_device(): grad_slab = lax.all_gather(grad_hidden, 'rep', axis=0, tiled=True)]
    all_to_all x0 -> x1, waiting for transfers between devices: none -> 11 us  [on_device(): grad_slab = jnp.concatenate(lax.all_to_all(sent, 'rep', 0, 0), axis=0)]
    psum x1, waiting for transfers between devices: 218 us -> 209 us  [on_device(): grad_weight = lax.psum(weight_part, ('rep', 'blk'))]
  transfers between devices with their start and end apart: 5 -> 5, of which waited for: 5 -> 5; matrix products, arithmetic and copies ran while one was open for 6% -> 7% of each run, Pallas kernels for 0% -> 0%
where the time goes in v1:
time: 596 us; the launch traced here: 595 us
  waiting for transfers between devices  491 us (82%)
  local copies, waits for them, and re-layouts  48.9 us (8%)
  matrix products  33.9 us (6%)
  between operations  14.5 us (2%)
    psum x1, waiting for transfers between devices, on_device(): grad_weight = lax.psum(weight_part, ('rep', 'blk'))  209 us
    reduce_scatter x1, waiting for transfers between devices, on_device(): lax.psum_scatter(column_terms, 'blk', scatter_dimension=0, tiled=True)  125 us
    reduce_scatter x1, waiting for transfers between devices, on_device(): lax.psum_scatter(partial_value, 'rep', scatter_dimension=0, tiled=True)  76.1 us
    all_gather x1, waiting for transfers between devices, on_device(): gathered = lax.all_gather(node_features, 'blk', axis=0, tiled=True)  69.5 us
    dot_general x1, local copies, waits for them, and re-layouts, on_device(): jnp.einsum('tij,tif->tjf', tile_block, picked_rows, preferred_element_typ...  12.8 us
    dot_general x1, local copies, waits for them, and re-layouts, on_device(): jnp.einsum('tij,tjf->tif', tile_block, picked, preferred_element_type=jnp...  12.3 us
  transfers between devices with their start and end apart: 5, of which 5 were waited for; matrix products, arithmetic and copies ran while one was open for 7% of the time, Pallas kernels for 0%

profile of v1, /device:TPU:24, one launch (start us, length us, event | category | flops | bytes accessed | tf_op | source)
XLA Modules:
  0.0 595.0 jit_solution(171982931680560530)
XLA Ops:
  7.2 0.0 copy-start
  7.2 0.0 all-gather.2.cloned.1.call-start
  7.2 0.7 all-gather.2.cloned.1.call-update
  7.9 0.0 reduce-scatter.3.cloned.1.call-start
  8.6 0.7 fusion.32
  9.3 0.7 compare_and_fusion.1
  9.9 69.5 %all-gather.2.cloned.1.call-done = bf16[8192,256]{1,0:T(8,128)(2,1)} async-done(((bf16[256,256]{1,0:T(8,128)(2,1)}), bf16[8192,256]{1,0:T(8,128)(2,1)}) %all-gather.2.cloned.1.call-update) | async-done | bytes 4194320 | tf_op jit(solution)/shard_map/all_gather | solution.py:22
  79.4 8.8 %gather_fusion = bf16[128,128,256]{2,1,0:T(8,128)(2,1)} fusion(bf16[64,128,256]{2,1,0:T(8,128)(2,1)} %bitcast.51, s32[1024]{0:T(1024)S(1)} %pad_clamp_fusion.1), kind=kCustom, calls=%fused_computation | custom fusion | bytes 16777728 | tf_op jit(solution)/shard_map/jit(_take)/gather | solution.py:28
  88.2 11.8 %fusion.6 = bf16[128,256,128]{2,1,0:T(8,128)(2,1)} fusion(bf16[128,128,256]{2,1,0:T(8,128)(2,1)} %gather_fusion, pred[128]{0:T(512)(128)(4,1)S(1)} %compare_and_fusion.1, bf16[1,1,128,128,128]{4,3,2,1,0:T(8,128)(2,1)} %param.8), kind=kOutput, calls=%fused_computation.8 | convolution fusion | flops 1077936128 | bytes 20971648 | tf_op jit(solution)/shard_map/tij,tjf->tif/dot_general | solution.py:29
  100.0 0.0 copy-start.2
  100.0 12.3 %copy.12 = bf16[128,256,128]{1,0,2:T(8,128)(2,1)} copy(bf16[128,256,128]{2,1,0:T(8,128)(2,1)} %fusion.6) | data formatting | bytes 16777216 | tf_op jit(solution)/shard_map/tij,tjf->tif/dot_general | solution.py:29
  112.3 0.0 copy-start.4
  112.3 0.0 copy-done.2
  112.3 4.6 fusion.17
  116.9 1.4 copy.10
  118.2 0.0 reduce-scatter.3.cloned.1.call-update
  118.3 76.1 %reduce-scatter.3.cloned.1.call-done = bf16[256,256]{1,0:T(8,128)(2,1)} async-done(((bf16[2048,256]{1,0:T(8,128)(2,1)}), bf16[256,256]{1,0:T(8,128)(2,1)}) %reduce-scatter.3.cloned.1.call-update) | async-done | bytes 131088 | tf_op jit(solution)/shard_map/reduce_scatter | solution.py:36
  194.4 0.0 copy-done
  194.4 0.0 copy-done.4
  194.4 1.8 fusion.20
  196.2 0.2 convolution_convert_fusion
  196.5 1.0 stack.2
  197.5 5.4 all-to-all-start
  202.9 0.0 all-reduce.2.cloned.1.call-start
  202.9 1.8 fusion.38
  204.8 0.0 all-reduce.2.cloned.1.call-update
  204.8 0.2 reduce-scatter.5.cloned.1.call-start
  205.0 11.0 %all-to-all-done = bf16[8,256,256]{2,1,0:T(8,128)(2,1)S(1)} async-done(((bf16[8,256,256]{2,1,0:T(8,128)(2,1)}), bf16[8,256,256]{2,1,0:T(8,128)(2,1)S(1)}, u32[]{:S(2)}, u32[]{:S(2)}) %all-to-all-start) | async-done | bytes 1048608 | tf_op jit(solution)/shard_map/all_to_all | solution.py:50
  216.0 6.6 %gather_fusion.1 = bf16[128,128,256]{2,1,0:T(8,128)(2,1)} fusion(bf16[16,128,256]{2,1,0:T(8,128)(2,1)S(1)} %bitcast.50, s32[1024]{0:T(1024)S(1)} %pad_clamp_fusion), kind=kCustom, calls=%fused_computation.1 | custom fusion | bytes 16777728 | tf_op jit(solution)/shard_map/jit(_take)/gather | solution.py:53
  222.6 8.8 %fusion.4 = bf16[128,256,128]{2,1,0:T(8,128)(2,1)} fusion(bf16[128,128,256]{2,1,0:T(8,128)(2,1)} %gather_fusion.1, pred[128]{0:T(512)(128)(4,1)S(1)} %compare_and_fusion, bf16[1,1,128,128,128]{4,3,2,1,0:T(8,128)(2,1)} %param.8), kind=kOutput, calls=%fused_computation.6 | convolution fusion | flops 1077936128 | bytes 20971648 | tf_op jit(solution)/shard_map/tij,tif->tjf/dot_general | solution.py:54
  231.4 0.0 copy-start.3
  231.4 12.8 %copy.13 = bf16[128,256,128]{1,0,2:T(8,128)(2,1)} copy(bf16[128,256,128]{2,1,0:T(8,128)(2,1)} %fusion.4) | data formatting | bytes 16777216 | tf_op jit(solution)/shard_map/tij,tif->tjf/dot_general | solution.py:54
  244.3 0.0 copy-done.3
  244.3 0.0 copy-start.1
  244.3 4.7 fusion.14
  249.0 4.4 copy.11
  253.4 0.0 reduce-scatter.5.cloned.1.call-update
  253.4 208.6 %all-reduce.2.cloned.1.call-done = f32[256,256]{1,0:T(8,128)} async-done(((f32[256,256]{1,0:T(8,128)}), f32[256,256]{1,0:T(8,128)}) %all-reduce.2.cloned.1.call-update) | async-done | bytes 262160 | tf_op jit(solution)/shard_map/psum | solution.py:51
  462.0 124.8 %reduce-scatter.5.cloned.1.call-done = bf16[256,256]{1,0:T(8,128)(2,1)} async-done(((bf16[8192,256]{1,0:T(8,128)(2,1)}), bf16[256,256]{1,0:T(8,128)(2,1)}) %reduce-scatter.5.cloned.1.call-update) | async-done | bytes 131088 | tf_op jit(solution)/shard_map/reduce_scatter | solution.py:63
  586.8 1.7 copy.16
  588.5 0.0 copy-done.1
  (5 shorter events, 0.0 us)
Async XLA Ops:
  7.2 187.2 %copy-start = (bf16[256,256]{1,0:T(8,128)(2,1)S(1)}, bf16[256,256]{1,0:T(8,128)(2,1)}, u32[]{:S(2)}) copy-start(bf16[256,256]{1,0:T(8,128)(2,1)} %param.12) | copy-start | bytes 393220
  7.2 72.2 %all-gather.2.cloned.1.call-start = ((), (), s32[]{:S(2)}) async-start(), calls=%async_computation.3 | async-start | bytes 4325376 | tf_op jit(solution)/shard_map/all_gather | solution.py:22
  7.9 186.5 %reduce-scatter.3.cloned.1.call-start = ((), (), s32[]{:S(2)}) async-start(), calls=%async_computation.4 | async-start | bytes 1179648 | tf_op jit(solution)/shard_map/reduce_scatter | solution.py:36
  100.0 12.3 %copy-start.2 = (s32[1,1,128]{2,1,0:T(1,128)S(1)}, s32[1,1,128]{2,1,0:T(1,128)}, u32[]{:S(2)}) copy-start(s32[1,1,128]{2,1,0:T(1,128)} %param.9) | copy-start | bytes 1540
  112.3 82.1 %copy-start.4 = (bf16[1,1,256,256]{3,2,1,0:T(8,128)(2,1)S(1)}, bf16[1,1,256,256]{3,2,1,0:T(8,128)(2,1)}, u32[]{:S(2)}) copy-start(bf16[1,1,256,256]{3,2,1,0:T(8,128)(2,1)} %param.13) | copy-start | bytes 393220
  197.5 18.5 %all-to-all-start = ((bf16[8,256,256]{2,1,0:T(8,128)(2,1)}), bf16[8,256,256]{2,1,0:T(8,128)(2,1)S(1)}, u32[]{:S(2)}, u32[]{:S(2)}) async-start(bf16[8,256,256]{2,1,0:T(8,128)(2,1)} %stack.2), calls=%async_computation.1 | async-start | bytes 2097152 | tf_op jit(solution)/shard_map/all_to_all | solution.py:50
  202.9 259.2 %all-reduce.2.cloned.1.call-start = ((), (), s32[]{:S(2)}) async-start(), calls=%async_computation.5 | async-start | bytes 524288 | tf_op jit(solution)/shard_map/psum | solution.py:51
  204.8 382.1 %reduce-scatter.5.cloned.1.call-start = ((), (), s32[]{:S(2)}) async-start(), calls=%async_computation.6 | async-start | bytes 4325376 | tf_op jit(solution)/shard_map/reduce_scatter | solution.py:63
  231.4 12.8 %copy-start.3 = (s32[1,1,128]{2,1,0:T(1,128)S(1)}, s32[1,1,128]{2,1,0:T(1,128)}, u32[]{:S(2)}) copy-start(s32[1,1,128]{2,1,0:T(1,128)} %param.10) | copy-start | bytes 1540
  244.3 344.3 %copy-start.1 = (bf16[256,256]{1,0:T(8,128)(2,1)S(1)}, bf16[256,256]{1,0:T(8,128)(2,1)}, u32[]{:S(2)}) copy-start(bf16[256,256]{1,0:T(8,128)(2,1)} %param.12) | copy-start | bytes 393220
Sparse Core Ops, SparseCore 0:
  9.9 69.5 all-gather.1
  118.4 75.9 reduce-scatter.2
  210.6 251.3 all-reduce.1
  465.2 121.6 reduce-scatter.4
